TPU v7x, 512 devices: a whole 4x4x16 slice. The times are simulated.
512 devices in a mesh: head: 8 (over y, x_hi), seq: 64 (over z, x_lo, core).
Axes of the slice: x: 4 (x_hi: 2, x_lo: 2; x = x_hi * 2 + x_lo), y: 4, z: 16, core: 2. Of those that a mesh axis runs over, the one named last changes fastest.
Arguments:
- tokens: bfloat16 [49152, 2048], P('seq', 'head'), may hold values from -6 to 6
- weights: bfloat16 [3, 2048, 2048], P(None, 'seq', 'head'), may hold values from -0.06591797 to 0.06591797
- landmark_pos: int32 [16, 256], P('head'), may hold values from 0 to 49151, as said below
Outputs:
- attended: bfloat16 [49152, 2048], P('seq', 'head')
Inputs may be any that keep to these rules, and one draw needn't show every extreme that they name: `landmark_pos`: landmark number j of every head lies in tokens j * 192 to (j + 1) * 192 - 1.
All inputs are finite; a program needn't handle non-finite values. Where the computation divides by a largest or mean magnitude, that divisor is 1e-20 or more.
Results may differ from a plain program's by a relative error of at most 0.0041.
Values may be sent and summed in bfloat16 or wider, within the bound.
No kernel may reach another device: no remote copies, remote signals or barrier semaphores. Data moves between devices by JAX's collectives and lax.ppermute only.
A program may use at most 64 MiB of HBM per device.

v0:
```python
import math
import jax
import jax.numpy as jnp
from jax import lax
from jax.sharding import PartitionSpec as P

NSTEPS = 6


def gauss(left, right):
    inner = jnp.einsum("hie,hje->hij", left, right, preferred_element_type=jnp.float32)
    left32 = left.astype(jnp.float32)
    right32 = right.astype(jnp.float32)
    dist = (
        jnp.sum(left32 * left32, -1)[:, :, None]
        + jnp.sum(right32 * right32, -1)[:, None, :]
        - 2.0 * inner
    )
    return jnp.exp(-dist / (2.0 * math.sqrt(left.shape[-1])))


def batched(left, right):
    return jnp.einsum("hij,hjk->hik", left, right, precision=lax.Precision.HIGHEST)


def gather_landmarks(query, keys, landmark_pos):
    per_group = landmark_pos.shape[1] // lax.axis_size("seq")
    tok_rows = query.shape[1]
    group = lax.axis_index("seq")
    local_pos = lax.dynamic_slice_in_dim(landmark_pos, group * per_group, per_group, 1)
    offsets = local_pos - group * tok_rows
    picker = (offsets[:, :, None] == jnp.arange(tok_rows, dtype=jnp.int32)[None, None, :]).astype(
        jnp.bfloat16
    )
    picked_q = jnp.einsum("hjt,hte->hje", picker, query, preferred_element_type=jnp.float32)
    picked_k = jnp.einsum("hjt,hte->hje", picker, keys, preferred_element_type=jnp.float32)
    number = group * per_group + jnp.arange(per_group, dtype=jnp.int32)
    even = (number % 2 == 0)[None, :, None]
    local_marks = jnp.where(even, picked_q, picked_k).astype(jnp.bfloat16)
    return lax.all_gather(local_marks, "seq", axis=1, tiled=True)


def shards(tokens, weights, landmark_pos):
    tok_rows = tokens.shape[0]
    heads_dev = landmark_pos.shape[0]
    head_cols = weights.shape[2]
    head_size = head_cols // heads_dev
    whole = lax.all_gather(tokens, "head", axis=1, tiled=True)

    def heads_of(flat):
        return jnp.transpose(
            flat.astype(jnp.bfloat16).reshape(tok_rows, heads_dev, head_size), (1, 0, 2)
        )

    projected = jnp.einsum(
        "td,kdc->ktc",
        whole,
        lax.all_gather(weights, "seq", axis=1, tiled=True),
        preferred_element_type=jnp.float32,
    )
    query = heads_of(projected[0])
    keys = heads_of(projected[1])
    values = heads_of(projected[2])
    landmarks = gather_landmarks(query, keys, landmark_pos)
    key_weights = gauss(landmarks, keys).astype(jnp.bfloat16)
    partial_sum = jnp.einsum(
        "hjt,hte->hje", key_weights, values, preferred_element_type=jnp.float32
    )
    summary = lax.psum(partial_sum, "seq")
    inner = gauss(landmarks, landmarks)
    scale_cols = jnp.max(jnp.sum(jnp.abs(inner), 1), axis=-1)
    scale_rows = jnp.max(jnp.sum(jnp.abs(inner), 2), axis=-1)
    iterate = inner / (scale_cols * scale_rows)[:, None, None]
    for step in range(NSTEPS):
        iterate = 2.0 * iterate - batched(batched(iterate, inner), iterate)
    mixed = batched(iterate, summary).astype(jnp.bfloat16)
    query_weights = gauss(query, landmarks).astype(jnp.bfloat16)
    result = jnp.einsum("htm,hme->the", query_weights, mixed, preferred_element_type=jnp.float32)
    return result.reshape(tok_rows, head_cols).astype(jnp.bfloat16)


def solution(mesh):
    return jax.shard_map(
        shards,
        mesh=mesh,
        in_specs=(P("seq", "head"), P(None, "seq", "head"), P("head", None)),
        out_specs=P("seq", "head"),
        check_vma=False,
    )
```

profile of v0, /device:TPU:1, one launch (start us, length us, event | category | flops | bytes accessed | tf_op | source)
XLA Modules:
  0.0 707.9 jit_solution(10493289057307640920)
XLA Ops:
  6.5 0.0 all-gather.5.cloned.1.call-start
  6.5 0.7 all-gather.5.cloned.1.call-update
  7.3 0.0 all-gather.3.cloned.1.call-start
  7.3 0.7 all-gather.3.cloned.1.call-update
  8.0 0.0 all-reduce.2.cloned.1.call-start
  8.1 0.8 dynamic-slice_subtract_fusion
  8.8 85.7 %all-gather.5.cloned.1.call-done = bf16[768,2048]{1,0:T(8,128)(2,1)} async-done(((bf16[768,256]{1,0:T(8,128)(2,1)}), bf16[768,2048]{1,0:T(8,128)(2,1)}) %all-gather.5.cloned.1.call-update) | async-done | bytes 3145744 | tf_op jit(solution)/shard_map/all_gather | solution.py:48
  94.6 124.4 %all-gather.3.cloned.1.call-done = bf16[3,2048,256]{2,1,0:T(8,128)(2,1)} async-done(((bf16[3,32,256]{2,1,0:T(8,128)(2,1)}), bf16[3,2048,256]{2,1,0:T(8,128)(2,1)}) %all-gather.3.cloned.1.call-update) | async-done | bytes 3145744 | tf_op jit(solution)/shard_map/all_gather | solution.py:58
  219.0 5.5 fusion.5
  224.5 0.1 fusion.51
  224.6 0.2 copy.27
  224.8 0.3 multiply_reduce_fusion
  225.1 0.2 fusion.33
  225.3 0.2 copy.28
  225.6 0.3 multiply_reduce_fusion.1
  225.9 0.2 fusion.15
  226.1 62.3 %all_gather.11 = bf16[2,256,128]{2,0,1:T(2,128)(2,1)S(1)} all-gather(bf16[2,4,128]{2,0,1:T(2,128)(2,1)S(1)} %copy.29), channel_id=1, replica_groups=mesh['head'=8,'seq'=64] {'seq'}, dimensions={1}, use_global_device_ids=true | all-gather | bytes 133120 | tf_op jit(solution)/shard_map/all_gather | solution.py:40
  288.4 0.3 multiply_reduce_fusion.2
  288.7 0.1 copy.30
  288.8 0.4 fusion.50
  289.2 0.1 reduce_max.18
  289.4 0.1 reduce_max.19
  289.5 0.7 fusion.24
  290.2 0.8 convolution_subtract_fusion.5
  291.0 0.7 fusion.52
  291.6 0.7 convolution_subtract_fusion.4
  292.3 0.7 fusion.53
  293.0 0.7 convolution_subtract_fusion.3
  293.6 0.7 fusion.54
  294.3 0.7 convolution_subtract_fusion.2
  295.0 0.7 fusion.55
  295.6 0.7 convolution_subtract_fusion.1
  296.3 0.7 fusion.56
  297.0 0.2 copy.36
  297.2 1.5 fusion.8
  298.7 0.0 all-reduce.2.cloned.1.call-update
  298.7 0.7 convolution_subtract_fusion
  299.4 398.6 %all-reduce.2.cloned.1.call-done = f32[2,256,128]{2,1,0:T(8,128)} async-done(((f32[2,256,128]{2,1,0:T(8,128)}), f32[2,256,128]{2,1,0:T(8,128)}) %all-reduce.2.cloned.1.call-update) | async-done | bytes 262160 | tf_op jit(solution)/shard_map/psum | solution.py:69
  698.0 1.6 convolution_convert_fusion
  699.6 0.8 fusion.10
  700.4 0.9 copy.40
  (3 shorter events, 0.0 us)
Async XLA Ops:
  6.5 88.0 %all-gather.5.cloned.1.call-start = ((), (), s32[]{:S(2)}) async-start(), calls=%async_computation.1 | async-start | bytes 3538944 | tf_op jit(solution)/shard_map/all_gather | solution.py:48
  7.3 211.7 %all-gather.3.cloned.1.call-start = ((), (), s32[]{:S(2)}) async-start(), calls=%async_computation | async-start | bytes 3194880 | tf_op jit(solution)/shard_map/all_gather | solution.py:58
  8.0 690.0 %all-reduce.2.cloned.1.call-start = ((), (), s32[]{:S(2)}) async-start(), calls=%async_computation.2 | async-start | bytes 524288 | tf_op jit(solution)/shard_map/psum | solution.py:69
Sparse Core Ops, SparseCore 0:
  10.4 84.1 all-gather.4
  96.7 122.2 all-gather.2
  298.9 399.1 all-reduce.1
where the time goes:
time: 708 us
  waiting for transfers between devices  610 us (86%)
  blocking collectives  62.3 us (9%)
  matrix products  18.2 us (3%)
  between operations  13.3 us (2%)
    psum x1, waiting for transfers between devices, shards(): summary = lax.psum(partial_sum, 'seq')  399 us
    all_gather x1, waiting for transfers between devices, shards(): lax.all_gather(weights, 'seq', axis=1, tiled=True)  124 us
    all_gather x1, waiting for transfers between devices, shards(): whole = lax.all_gather(tokens, 'head', axis=1, tiled=True)  85.7 us
    all_gather x1, blocking collectives, gather_landmarks(): return lax.all_gather(local_marks, 'seq', axis=1, tiled=True)  62.3 us
  transfers between devices with their start and end apart: 3, of which 3 were waited for; matrix products, arithmetic and copies ran while one was open for 0% of the time, Pallas kernels for 0%

commit v1 on v0

--- a/solution.py
+++ b/solution.py
@@ -66,7 +66,7 @@
     partial_sum = jnp.einsum(
         "hjt,hte->hje", key_weights, values, preferred_element_type=jnp.float32
     )
-    summary = lax.psum(partial_sum, "seq")
+    summary = jax.lax.all_gather(partial_sum, "seq").sum(axis=0)
     inner = gauss(landmarks, landmarks)
     scale_cols = jnp.max(jnp.sum(jnp.abs(inner), 1), axis=-1)
     scale_rows = jnp.max(jnp.sum(jnp.abs(inner), 2), axis=-1)

time: 708 us -> 442 us (0.62)
  waiting for transfers between devices: 610 us -> 339 us
    psum x1 -> x0, waiting for transfers between devices: 399 us -> none  [shards(): summary = lax.psum(partial_sum, 'seq')]
    all_gather x0 -> x1, waiting for transfers between devices: none -> 127 us  [shards(): summary = jax.lax.all_gather(partial_sum, 'seq').sum(axis=0)]
  transfers between devices with their start and end apart: 3 -> 3, of which waited for: 3 -> 3; matrix products, arithmetic and copies ran while one was open for 0% -> 2% of each run, Pallas kernels for 0% -> 0%
where the time goes in v1:
time: 442 us
  waiting for transfers between devices  339 us (77%)
  blocking collectives  62.3 us (14%)
  matrix products  17.3 us (4%)
  between operations  13.3 us (3%)
  other arithmetic  8.5 us (2%)
    all_gather x1, waiting for transfers between devices, shards(): summary = jax.lax.all_gather(partial_sum, 'seq').sum(axis=0)  127 us
    all_gather x1, waiting for transfers between devices, shards(): lax.all_gather(weights, 'seq', axis=1, tiled=True)  124 us
    all_gather x1, waiting for transfers between devices, shards(): whole = lax.all_gather(tokens, 'head', axis=1, tiled=True)  85.7 us
    all_gather x1, blocking collectives, gather_landmarks(): return lax.all_gather(local_marks, 'seq', axis=1, tiled=True)  62.3 us
  transfers between devices with their start and end apart: 3, of which 3 were waited for; matrix products, arithmetic and copies ran while one was open for 2% of the time, Pallas kernels for 0%

profile of v1, /device:TPU:1, one launch (start us, length us, event | category | flops | bytes accessed | tf_op | source)
XLA Modules:
  0.0 442.0 jit_solution(5104217001340310524)
XLA Ops:
  6.5 0.0 all-gather.7.cloned.1.call-start
  6.5 0.7 all-gather.7.cloned.1.call-update
  7.3 0.0 all-gather.5.cloned.1.call-start
  7.3 0.7 all-gather.5.cloned.1.call-update
  8.0 0.0 all-gather.9.cloned.1.call-start
  8.1 0.8 dynamic-slice_subtract_fusion
  8.8 85.7 %all-gather.7.cloned.1.call-done = bf16[768,2048]{1,0:T(8,128)(2,1)} async-done(((bf16[768,256]{1,0:T(8,128)(2,1)}), bf16[768,2048]{1,0:T(8,128)(2,1)}) %all-gather.7.cloned.1.call-update) | async-done | bytes 3145744 | tf_op jit(solution)/shard_map/all_gather | solution.py:48
  94.6 124.4 %all-gather.5.cloned.1.call-done = bf16[3,2048,256]{2,1,0:T(8,128)(2,1)} async-done(((bf16[3,32,256]{2,1,0:T(8,128)(2,1)}), bf16[3,2048,256]{2,1,0:T(8,128)(2,1)}) %all-gather.5.cloned.1.call-update) | async-done | bytes 3145744 | tf_op jit(solution)/shard_map/all_gather | solution.py:58
  219.0 5.5 %fusion.5 = bf16[3,768,256]{1,2,0:T(8,128)(2,1)S(1)} fusion(bf16[3,2048,256]{2,1,0:T(8,128)(2,1)} %all-gather.5.cloned.1.call-done, bf16[768,2048]{1,0:T(8,128)(2,1)} %all-gather.7.cloned.1.call-done), kind=kOutput, calls=%fused_computation.5 | convolution fusion | flops 2416508928 | bytes 7471104 | tf_op jit(solution)/shard_map/td,kdc->ktc/dot_general | solution.py:55
  224.5 0.1 fusion.51
  224.6 0.2 copy.29
  224.8 0.2 copy.30
  225.1 0.3 multiply_reduce_fusion.1
  225.4 0.2 fusion.33
  225.6 0.2 fusion.15
  225.8 62.3 %all_gather.17 = bf16[2,256,128]{2,0,1:T(2,128)(2,1)S(1)} all-gather(bf16[2,4,128]{2,0,1:T(2,128)(2,1)S(1)} %copy.31), channel_id=1, replica_groups=mesh['head'=8,'seq'=64] {'seq'}, dimensions={1}, use_global_device_ids=true | all-gather | bytes 133120 | tf_op jit(solution)/shard_map/all_gather | solution.py:40
  288.1 0.3 multiply_reduce_fusion.2
  288.5 0.1 copy.32
  288.5 0.2 copy.38
  288.8 1.5 fusion.8
  290.2 0.0 all-gather.9.cloned.1.call-update
  290.3 0.4 fusion.50
  290.7 0.1 reduce_max.18
  290.8 0.1 reduce_max.19
  290.9 0.3 multiply_reduce_fusion
  291.2 0.7 fusion.24
  291.9 0.8 convolution_subtract_fusion.5
  292.7 0.7 fusion.52
  293.3 0.7 convolution_subtract_fusion.4
  294.0 0.7 fusion.53
  294.7 0.7 convolution_subtract_fusion.3
  295.4 0.7 fusion.54
  296.0 0.7 convolution_subtract_fusion.2
  296.7 0.7 fusion.55
  297.4 0.7 convolution_subtract_fusion.1
  298.0 0.7 fusion.56
  298.7 0.7 convolution_subtract_fusion
  299.4 127.2 %all-gather.9.cloned.1.call-done = f32[128,256,128]{2,1,0:T(8,128)} async-done(((f32[2,256,128]{2,1,0:T(8,128)}), f32[128,256,128]{2,1,0:T(8,128)}) %all-gather.9.cloned.1.call-update) | async-done | bytes 16777232 | tf_op jit(solution)/shard_map/all_gather | solution.py:69
  426.6 6.6 %reduce_sum.58 = f32[2,256,128]{2,1,0:T(8,128)S(1)} reduce(f32[64,2,256,128]{3,2,1,0:T(8,128)} %bitcast.59, f32[]{:T(128)} %constant.38.clone.1), dimensions={0}, to_apply=%region_6.7 | reduce | flops 4128768 | bytes 17039364 | tf_op jit(solution)/shard_map/reduce_sum | solution.py:69
  433.1 0.6 convolution_convert_fusion
  433.7 0.8 fusion.10
  434.5 0.9 copy.42
  (3 shorter events, 0.0 us)
Async XLA Ops:
  6.5 88.0 %all-gather.7.cloned.1.call-start = ((), (), s32[]{:S(2)}) async-start(), calls=%async_computation.1 | async-start | bytes 3538944 | tf_op jit(solution)/shard_map/all_gather | solution.py:48
  7.3 211.7 %all-gather.5.cloned.1.call-start = ((), (), s32[]{:S(2)}) async-start(), calls=%async_computation | async-start | bytes 3194880 | tf_op jit(solution)/shard_map/all_gather | solution.py:58
  8.0 418.6 %all-gather.9.cloned.1.call-start = ((), (), s32[]{:S(2)}) async-start(), calls=%async_computation.2 | async-start | bytes 17039360 | tf_op jit(solution)/shard_map/all_gather | solution.py:69
Sparse Core Ops, SparseCore 0:
  10.4 84.1 all-gather.6
  96.7 122.2 all-gather.4
  290.4 136.1 all-gather.8
